TPU v7x, 32 devices: a whole 2x2x4 slice. The times are simulated.
32 devices in a mesh: pole: 4 (over z), row: 4 (over y, x), col: 2 (over core).
Axes of the slice: x: 2, y: 2, z: 4, core: 2. Of those that a mesh axis runs over, the one named last changes fastest.
Arguments:
- green_blocks: bfloat16 [16, 2, 192, 1536], P('pole', 'col', None, 'row'), parts along dimension 0, may hold values from -0.15625 to 0.15625
- lower_panel: bfloat16 [1536, 32, 128], P(('row', 'col'), 'pole'), parts along dimension 1, may hold values from -1.5 to 1.5
- pattern: int32 [12, 8], replicated, may hold values 0 or 1
- pivot_inverse: float32 [8, 512, 128], P(('row', 'col'), 'pole'), parts along dimension 1, may hold values from -6 to 6
Outputs:
- green_panel: bfloat16 [6144, 8, 128], P('pole', ('row', 'col')), parts along dimension 0
- green_diag: float32 [8, 512, 128], P(('row', 'col'), 'pole'), parts along dimension 1
There are 4 independent parts, one for each index of `pole`. A program takes and returns all parts, laid end to end along the dimension named above; an argument that names none is the same for every part. Nothing has to cross between parts.
All inputs are finite; a program needn't handle non-finite values.
Results may differ from a plain program's by a relative error of at most 0.01.
Values may be sent and summed in bfloat16 or wider, within the bound.
A program may use at most 128 MiB of HBM per device.

v0:
```python
import jax
import jax.numpy as jnp
from jax import lax
from jax.sharding import PartitionSpec as P


def local(green_blocks, lower_panel, pattern, pivot_inverse):
    row_count = lax.axis_size("row")
    col_count = lax.axis_size("col")
    row_share, supernodes, width = lower_panel.shape
    block_count = pattern.shape[0]
    position = lax.axis_index("row") * col_count + lax.axis_index("col")
    row_ids = position * row_share + jnp.arange(row_share, dtype=jnp.int32)
    onehot = (
        row_ids[:, None] // width == jnp.arange(block_count, dtype=jnp.int32)[None, :]
    ).astype(jnp.float32)
    own_mask = jnp.dot(onehot, pattern.astype(jnp.float32), precision=lax.Precision.HIGHEST)
    masked = lower_panel * own_mask[:, :, None].astype(jnp.bfloat16)
    local_green = green_blocks.reshape(-1, green_blocks.shape[3])
    piece = lax.all_gather(masked, "col", axis=0, tiled=True)
    partial_value = jnp.dot(
        local_green, piece.reshape(piece.shape[0], -1), preferred_element_type=jnp.float32
    )
    shaped = partial_value.astype(jnp.bfloat16).reshape(partial_value.shape[0], supernodes, width)
    received = lax.all_to_all(shaped, ("row", "col"), split_axis=1, concat_axis=0, tiled=True)
    kept = received.shape[1]
    received = received.reshape(row_count, col_count, row_count, row_share, kept, width)
    resolved = (
        jnp.sum(received.astype(jnp.float32), axis=0)
        .transpose(1, 0, 2, 3, 4)
        .reshape(-1, kept, width)
    )
    column_panel = lax.all_to_all(masked, ("row", "col"), split_axis=1, concat_axis=0, tiled=True)
    own_columns = lax.dynamic_slice_in_dim(pattern, position * kept, kept, 1)
    column_mask = jnp.repeat(own_columns, width, axis=0).astype(jnp.float32)
    green_panel = (-(resolved * column_mask[:, :, None])).astype(jnp.bfloat16)
    green_diag = pivot_inverse + jnp.einsum(
        "rkb,rkc->kbc", column_panel.astype(jnp.float32), resolved, precision=lax.Precision.HIGHEST
    )
    return (green_panel, green_diag)


def solution(mesh):
    placed = (
        P("pole", "col", None, "row"),
        P(("row", "col"), "pole", None),
        P(),
        P(("row", "col"), "pole", None),
    )
    return jax.shard_map(
        local,
        mesh=mesh,
        in_specs=placed,
        out_specs=(P("pole", ("row", "col"), None), P(("row", "col"), "pole", None)),
        check_vma=False,
    )
```

profile of v0, /device:TPU:0, one launch (start us, length us, event | category | flops | bytes accessed | tf_op | source)
XLA Modules:
  0.0 47.8 jit_solution(6955600791728680446)
XLA Ops:
  0.6 0.0 copy-start
  0.7 0.9 %convolution_convert_fusion.1 = bf16[192,8]{0,1:T(8,128)(2,1)S(1)} fusion(s32[192]{0:T(256)S(1)} %and_select_fusion, s32[12,8]{0,1:T(8,128)} %param.6), kind=kOutput, calls=%fused_computation.4 | convolution fusion | flops 225120 | bytes 4224 | tf_op jit(solution)/shard_map/dot_general | solution.py:17
  1.6 0.2 copy.16
  1.8 1.3 %broadcast_multiply_fusion = bf16[192,8,128]{2,1,0:T(8,128)(2,1)S(1)} fusion(bf16[192,8,128]{2,1,0:T(8,128)(2,1)} %param.5, bf16[192,8]{1,0:T(8,128)(2,1)S(1)} %copy.16), kind=kLoop, calls=%fused_computation.8 | loop fusion | flops 196608 | bytes 789504 | tf_op jit(solution)/shard_map/mul | solution.py:18
  3.1 2.5 %all_gather.3 = bf16[384,8,128]{2,1,0:T(8,128)(2,1)S(1)} all-gather(bf16[192,8,128]{2,1,0:T(8,128)(2,1)S(1)} %broadcast_multiply_fusion), channel_id=1, replica_groups=mesh['pole'=4,'row'=4,'col'=2] {'col'}, dimensions={0}, use_global_device_ids=true | all-gather | bytes 1179648 | tf_op jit(solution)/shard_map/all_gather | solution.py:20
  5.6 0.6 %copy.17 = bf16[384,8,128]{0,2,1:T(8,128)(2,1)S(1)} copy(bf16[384,8,128]{2,1,0:T(8,128)(2,1)S(1)} %all_gather.3) | data formatting | bytes 1572864 | tf_op jit(solution)/shard_map/all_gather | solution.py:20
  6.2 0.0 copy-done
  6.2 1.0 %convolution_convert_fusion = bf16[1024,768]{1,0:T(8,128)(2,1)S(1)} fusion(bf16[384,1024]{0,1:T(8,128)(2,1)S(1)} %bitcast.44, bf16[768,384]{1,0:T(8,128)(2,1)S(1)} %bitcast.38), kind=kOutput, calls=%fused_computation | convolution fusion | flops 604766208 | bytes 2949120 | tf_op jit(solution)/shard_map/dot_general | solution.py:21
  7.2 1.6 %copy.18 = bf16[768,8,128]{2,0,1:T(8,128)(2,1)} copy(bf16[768,8,128]{0,2,1:T(8,128)(2,1)S(1)} %bitcast.42) | data formatting | bytes 3145728 | tf_op jit(solution)/shard_map/reshape | solution.py:24
  8.8 5.1 %all-to-all-start = ((bf16[768,8,128]{2,0,1:T(8,128)(2,1)}), bf16[768,8,128]{2,0,1:T(8,128)(2,1)S(1)}, u32[]{:S(2)}, u32[]{:S(2)}) async-start(bf16[768,8,128]{2,0,1:T(8,128)(2,1)} %copy.18), calls=%async_computation | async-start | bytes 3145728 | tf_op jit(solution)/shard_map/all_to_all | solution.py:25
  13.8 0.8 %copy.20 = bf16[192,8,128]{2,0,1:T(8,128)(2,1)} copy(bf16[192,8,128]{2,1,0:T(8,128)(2,1)S(1)} %broadcast_multiply_fusion) | data formatting | bytes 786432 | tf_op jit(solution)/shard_map/mul | solution.py:18
  14.7 0.7 %convert_bitcast_fusion = f32[12]{0:T(128)S(1)} fusion(s32[12,8]{0,1:T(8,128)} %param.6, s32[]{:T(128)S(6)} %select_n.14), kind=kLoop, calls=%fused_computation.17 | loop fusion | flops 12 | bytes 100 | tf_op jit(solution)/shard_map/convert_element_type | solution.py:35
  15.3 0.1 broadcast_bitcast_fusion
  15.4 19.4 %all-to-all-done = bf16[768,8,128]{2,0,1:T(8,128)(2,1)S(1)} async-done(((bf16[768,8,128]{2,0,1:T(8,128)(2,1)}), bf16[768,8,128]{2,0,1:T(8,128)(2,1)S(1)}, u32[]{:S(2)}, u32[]{:S(2)}) %all-to-all-start) | async-done | bytes 1572896 | tf_op jit(solution)/shard_map/all_to_all | solution.py:25
  34.8 3.5 %all-to-all-start.1 = ((bf16[192,8,128]{2,0,1:T(8,128)(2,1)}), bf16[192,8,128]{2,0,1:T(8,128)(2,1)S(1)}, u32[]{:S(2)}, u32[]{:S(2)}) async-start(bf16[192,8,128]{2,0,1:T(8,128)(2,1)} %copy.20), calls=%async_computation.1 | async-start | bytes 786432 | tf_op jit(solution)/shard_map/all_to_all | solution.py:33
  38.3 1.9 %bitcast_convert_fusion = f32[768,8,1,128]{3,0,1,2:T(8,128)} fusion(bf16[768,8,128]{2,0,1:T(8,128)(2,1)S(1)} %all-to-all-done), kind=kLoop, calls=%fused_computation.1 | loop fusion | flops 786432 | bytes 4718592 | tf_op jit(solution)/shard_map/convert_element_type | solution.py:29
  40.1 2.1 %reduce_sum.11 = f32[2,4,192,128]{3,2,1,0:T(8,128)S(1)} reduce(f32[4,2,4,192,128]{4,3,2,1,0:T(8,128)} %bitcast.39, f32[]{:T(128)} %constant.31.clone.1), dimensions={0}, to_apply=%region_0.1 | reduce | flops 589824 | bytes 3932164 | tf_op jit(solution)/shard_map/reduce_sum | solution.py:29
  42.3 0.0 copy-start.1
  42.3 0.1 copy.19
  42.4 1.0 %fusion.2 = bf16[1536,1,128]{2,0,1:T(8,128)(2,1)} fusion(f32[4,2,192,1,128]{4,2,1,0,3:T(8,128)S(1)} %copy.19, f32[1536]{0:T(1024)S(1)} %broadcast_bitcast_fusion), kind=kLoop, calls=%fused_computation.7 | loop fusion | flops 589824 | bytes 1185792 | tf_op jit(solution)/shard_map/convert_element_type | solution.py:36
  43.4 3.1 %all-to-all-done.1 = bf16[192,8,128]{2,0,1:T(8,128)(2,1)S(1)} async-done(((bf16[192,8,128]{2,0,1:T(8,128)(2,1)}), bf16[192,8,128]{2,0,1:T(8,128)(2,1)S(1)}, u32[]{:S(2)}, u32[]{:S(2)}) %all-to-all-start.1) | async-done | bytes 393248 | tf_op jit(solution)/shard_map/all_to_all | solution.py:33
  46.5 0.0 copy-done.1
  46.5 1.2 %fusion = f32[1,128,128]{2,1,0:T(8,128)} fusion(f32[1,128,128]{2,1,0:T(8,128)S(1)} %copy-done.1, bf16[1536,128]{1,0:T(8,128)(2,1)S(1)} %bitcast.43, f32[1536,128]{1,0:T(8,128)S(1)} %bitcast.40), kind=kOutput, calls=%fused_computation.3 | convolution fusion | flops 302006272 | bytes 1310720 | tf_op jit(solution)/shard_map/rkb,rkc->kbc/dot_general | solution.py:37
  (1 shorter events, 0.0 us)
Async XLA Ops:
  0.6 5.5 %copy-start = (bf16[4,1,192,384]{3,2,1,0:T(8,128)(2,1)S(1)}, bf16[4,1,192,384]{3,2,1,0:T(8,128)(2,1)}, u32[]{:S(2)}) copy-start(bf16[4,1,192,384]{3,2,1,0:T(8,128)(2,1)} %param.4) | copy-start | bytes 1769476
  8.8 26.1 %all-to-all-start = ((bf16[768,8,128]{2,0,1:T(8,128)(2,1)}), bf16[768,8,128]{2,0,1:T(8,128)(2,1)S(1)}, u32[]{:S(2)}, u32[]{:S(2)}) async-start(bf16[768,8,128]{2,0,1:T(8,128)(2,1)} %copy.18), calls=%async_computation | async-start | bytes 3145728 | tf_op jit(solution)/shard_map/all_to_all | solution.py:25
  34.8 11.7 %all-to-all-start.1 = ((bf16[192,8,128]{2,0,1:T(8,128)(2,1)}), bf16[192,8,128]{2,0,1:T(8,128)(2,1)S(1)}, u32[]{:S(2)}, u32[]{:S(2)}) async-start(bf16[192,8,128]{2,0,1:T(8,128)(2,1)} %copy.20), calls=%async_computation.1 | async-start | bytes 786432 | tf_op jit(solution)/shard_map/all_to_all | solution.py:33
  42.3 4.2 %copy-start.1 = (f32[1,128,128]{2,1,0:T(8,128)S(1)}, f32[1,128,128]{2,1,0:T(8,128)}, u32[]{:S(2)}) copy-start(f32[1,128,128]{2,1,0:T(8,128)} %param.7) | copy-start | bytes 196612
where the time goes:
time: 48.2 us; the launch traced here: 47.8 us
  waiting for transfers between devices  22.6 us (47%)
  starting transfers between devices  8.53 us (18%)
  other arithmetic  6.99 us (15%)
  local copies, waits for them, and re-layouts  3.3 us (7%)
  matrix products  3.18 us (7%)
  blocking collectives  2.49 us (5%)
  between operations  0.71 us (1%)
    all_to_all x1, waiting for transfers between devices, local(): lax.all_to_all(shaped, ('row', 'col'), split_axis=1, concat_axis=0, tiled...  19.4 us
    all_to_all x1, starting transfers between devices, local(): lax.all_to_all(shaped, ('row', 'col'), split_axis=1, concat_axis=0, tiled...  5.08 us
    all_to_all x1, starting transfers between devices, local(): lax.all_to_all(masked, ('row', 'col'), split_axis=1, concat_axis=0, tiled...  3.45 us
    all_to_all x1, waiting for transfers between devices, local(): lax.all_to_all(masked, ('row', 'col'), split_axis=1, concat_axis=0, tiled...  3.15 us
    all_gather x1, blocking collectives, local(): piece = lax.all_gather(masked, 'col', axis=0, tiled=True)  2.49 us
    reduce_sum x1, other arithmetic, local(): jnp.sum(received.astype(jnp.float32), axis=0).transpose(1, 0, 2, 3, 4)  2.14 us
    convert_element_type x1, other arithmetic, local(): received.astype(jnp.float32)  1.86 us
    reshape x1, local copies, waits for them, and re-layouts, local(): partial_value.astype(jnp.bfloat16)  1.57 us
  transfers between devices with their start and end apart: 2, of which 2 were waited for; matrix products, arithmetic and copies ran while one was open for 14% of the time, Pallas kernels for 0%

commit v1 on v0

--- a/solution.py
+++ b/solution.py
@@ -1,7 +1,25 @@
+import functools
 import jax
 import jax.numpy as jnp
 from jax import lax
 from jax.sharding import PartitionSpec as P
+from jax.lax import all_to_all, axis_size
+
+
+def read_the_local_data(t0, mesh_ax):
+    state_now = jnp.concatenate(
+        all_to_all(
+            jnp.stack(jnp.split(t0, axis_size(mesh_ax), axis=1), axis=0),
+            axis_name=mesh_ax,
+            split_axis=0,
+            concat_axis=0,
+        ),
+        axis=0,
+    )
+    return state_now
+
+
+shape_the_screen = functools.partial(read_the_local_data, mesh_ax=("row", "col"))
 
 
 def local(green_blocks, lower_panel, pattern, pivot_inverse):
@@ -22,7 +40,7 @@
         local_green, piece.reshape(piece.shape[0], -1), preferred_element_type=jnp.float32
     )
     shaped = partial_value.astype(jnp.bfloat16).reshape(partial_value.shape[0], supernodes, width)
-    received = lax.all_to_all(shaped, ("row", "col"), split_axis=1, concat_axis=0, tiled=True)
+    received = shape_the_screen(shaped)
     kept = received.shape[1]
     received = received.reshape(row_count, col_count, row_count, row_share, kept, width)
     resolved = (

time: 48.2 us -> 53.6 us (1.11)
  local copies, waits for them, and re-layouts: 3.3 us -> 8.71 us
  other arithmetic: 6.99 us -> 3.23 us
  waiting for transfers between devices: 22.6 us -> 26.3 us
    unnamed x4 -> x19, local copies, waits for them, and re-layouts: 0.02 us -> 6.2 us
    all_to_all x1, waiting for transfers between devices: 3.15 us -> 6.91 us  [local(): lax.all_to_all(masked, ('row', 'col'), split_axis=1, concat_axis=0, tiled...]
    reduce_sum x1, other arithmetic: 2.14 us -> 0.24 us  [local(): jnp.sum(received.astype(jnp.float32), axis=0).transpose(1, 0, 2, 3, 4)]
    convert_element_type x1 -> x0, other arithmetic: 1.86 us -> none  [local(): received.astype(jnp.float32)]
    reshape x1 -> x0, local copies, waits for them, and re-layouts: 1.57 us -> none  [local(): partial_value.astype(jnp.bfloat16)]
    another operation x0 -> x1, local copies, waits for them, and re-layouts: none -> 0.7 us  [read_the_local_data(): jnp.stack(jnp.split(t0, axis_size(mesh_ax), axis=1), axis=0)]
  transfers between devices with their start and end apart: 2 -> 2, of which waited for: 2 -> 2; matrix products, arithmetic and copies ran while one was open for 14% -> 5% of each run, Pallas kernels for 0% -> 0%
where the time goes in v1:
time: 53.6 us; the launch traced here: 53.2 us
  waiting for transfers between devices  26.3 us (49%)
  local copies, waits for them, and re-layouts  8.71 us (16%)
  starting transfers between devices  8.53 us (16%)
  other arithmetic  3.23 us (6%)
  matrix products  3.18 us (6%)
  blocking collectives  2.49 us (5%)
  between operations  0.75 us (1%)
    all_to_all x1, waiting for transfers between devices, read_the_local_data(): all_to_all(jnp.stack(jnp.split(t0, axis_size(mesh_ax), axis=1), axis=0),...  19.4 us
    all_to_all x1, waiting for transfers between devices, local(): lax.all_to_all(masked, ('row', 'col'), split_axis=1, concat_axis=0, tiled...  6.91 us
    unnamed x19, local copies, waits for them, and re-layouts  6.2 us
    all_to_all x1, starting transfers between devices, read_the_local_data(): all_to_all(jnp.stack(jnp.split(t0, axis_size(mesh_ax), axis=1), axis=0),...  5.08 us
    all_to_all x1, starting transfers between devices, local(): lax.all_to_all(masked, ('row', 'col'), split_axis=1, concat_axis=0, tiled...  3.45 us
    all_gather x1, blocking collectives, local(): piece = lax.all_gather(masked, 'col', axis=0, tiled=True)  2.49 us
    mul x1, other arithmetic, local(): masked = lower_panel * own_mask[:, :, None].astype(jnp.bfloat16)  1.27 us
    dot_general x1, matrix products, local(): jnp.einsum('rkb,rkc->kbc', column_panel.astype(jnp.float32), resolved, pr...  1.24 us
  transfers between devices with their start and end apart: 2, of which 2 were waited for; matrix products, arithmetic and copies ran while one was open for 5% of the time, Pallas kernels for 0%

profile of v1, /device:TPU:0, one launch (start us, length us, event | category | flops | bytes accessed | tf_op | source)
XLA Modules:
  0.0 53.2 jit_solution(14417504523528083772)
XLA Ops:
  0.7 0.9 %convolution_convert_fusion.1 = bf16[192,8]{0,1:T(8,128)(2,1)S(1)} fusion(s32[192]{0:T(256)S(1)} %and_select_fusion, s32[12,8]{0,1:T(8,128)} %param.6), kind=kOutput, calls=%fused_computation.4 | convolution fusion | flops 225120 | bytes 4224 | tf_op jit(solution)/shard_map/dot_general | solution.py:35
  1.6 0.2 copy.38
  1.8 1.3 %broadcast_multiply_fusion = bf16[192,8,128]{2,1,0:T(8,128)(2,1)S(1)} fusion(bf16[192,8,128]{2,1,0:T(8,128)(2,1)} %param.5, bf16[192,8]{1,0:T(8,128)(2,1)S(1)} %copy.38), kind=kLoop, calls=%fused_computation.16 | loop fusion | flops 196608 | bytes 789504 | tf_op jit(solution)/shard_map/mul | solution.py:36
  3.1 2.5 %all_gather.3 = bf16[384,8,128]{2,1,0:T(8,128)(2,1)S(1)} all-gather(bf16[192,8,128]{2,1,0:T(8,128)(2,1)S(1)} %broadcast_multiply_fusion), channel_id=1, replica_groups=mesh['pole'=4,'row'=4,'col'=2] {'col'}, dimensions={0}, use_global_device_ids=true | all-gather | bytes 1179648 | tf_op jit(solution)/shard_map/all_gather | solution.py:38
  5.6 0.6 %copy.39 = bf16[384,8,128]{0,2,1:T(8,128)(2,1)S(1)} copy(bf16[384,8,128]{2,1,0:T(8,128)(2,1)S(1)} %all_gather.3) | data formatting | bytes 1572864 | tf_op jit(solution)/shard_map/all_gather | solution.py:38
  6.2 1.0 %convolution_convert_fusion = bf16[1024,768]{1,0:T(8,128)(2,1)S(1)} fusion(bf16[384,1024]{0,1:T(8,128)(2,1)S(1)} %bitcast.58, bf16[768,384]{1,0:T(8,128)(2,1)S(1)} %bitcast.52), kind=kOutput, calls=%fused_computation.1 | convolution fusion | flops 604766208 | bytes 2949120 | tf_op jit(solution)/shard_map/dot_general | solution.py:39
  7.2 0.1 fusion.5
  7.3 0.2 copy.52
  7.5 0.7 %bitcast_dynamic-update-slice_fusion.7 = bf16[8,768,1,128]{3,1,2,0:T(8,128)(2,1)} fusion(bf16[768,1,128]{2,0,1:T(8,128)(2,1)S(1)} %copy.52), kind=kLoop, calls=%fused_computation.15 | loop fusion | bytes 393216
  8.2 0.2 copy.53
  8.3 0.2 copy.54
  8.5 0.2 copy.55
  8.7 0.2 copy.56
  8.8 0.2 copy.57
  9.0 0.2 copy.58
  9.2 0.2 copy.59
  9.3 0.7 %bitcast_dynamic-update-slice_fusion.6 = bf16[8,768,1,128]{3,1,2,0:T(8,128)(2,1)} fusion(bf16[8,768,1,128]{3,1,2,0:T(8,128)(2,1)} %bitcast_dynamic-update-slice_fusion.7, bf16[768,1,128]{2,0,1:T(8,128)(2,1)S(1)} %copy.53), kind=kLoop, calls=%fused_computation.14 | loop fusion | bytes 393216
  10.0 0.7 %bitcast_dynamic-update-slice_fusion.5 = bf16[8,768,1,128]{3,1,2,0:T(8,128)(2,1)} fusion(bf16[8,768,1,128]{3,1,2,0:T(8,128)(2,1)} %bitcast_dynamic-update-slice_fusion.6, bf16[768,1,128]{2,0,1:T(8,128)(2,1)S(1)} %copy.54), kind=kLoop, calls=%fused_computation.13 | loop fusion | bytes 393216
  10.7 0.7 %bitcast_dynamic-update-slice_fusion.4 = bf16[8,768,1,128]{3,1,2,0:T(8,128)(2,1)} fusion(bf16[8,768,1,128]{3,1,2,0:T(8,128)(2,1)} %bitcast_dynamic-update-slice_fusion.5, bf16[768,1,128]{2,0,1:T(8,128)(2,1)S(1)} %copy.55), kind=kLoop, calls=%fused_computation.12 | loop fusion | bytes 393216
  11.4 0.7 %bitcast_dynamic-update-slice_fusion.3 = bf16[8,768,1,128]{3,1,2,0:T(8,128)(2,1)} fusion(bf16[8,768,1,128]{3,1,2,0:T(8,128)(2,1)} %bitcast_dynamic-update-slice_fusion.4, bf16[768,1,128]{2,0,1:T(8,128)(2,1)S(1)} %copy.56), kind=kLoop, calls=%fused_computation.11 | loop fusion | bytes 393216
  12.1 0.7 %bitcast_dynamic-update-slice_fusion.2 = bf16[8,768,1,128]{3,1,2,0:T(8,128)(2,1)} fusion(bf16[8,768,1,128]{3,1,2,0:T(8,128)(2,1)} %bitcast_dynamic-update-slice_fusion.3, bf16[768,1,128]{2,0,1:T(8,128)(2,1)S(1)} %copy.57), kind=kLoop, calls=%fused_computation.10 | loop fusion | bytes 393216
  12.8 0.7 %bitcast_dynamic-update-slice_fusion.1 = bf16[8,768,1,128]{3,1,2,0:T(8,128)(2,1)} fusion(bf16[8,768,1,128]{3,1,2,0:T(8,128)(2,1)} %bitcast_dynamic-update-slice_fusion.2, bf16[768,1,128]{2,0,1:T(8,128)(2,1)S(1)} %copy.58), kind=kLoop, calls=%fused_computation.9 | loop fusion | bytes 393216
  13.5 0.7 %bitcast_dynamic-update-slice_fusion = bf16[8,768,1,128]{3,1,2,0:T(8,128)(2,1)} fusion(bf16[8,768,1,128]{3,1,2,0:T(8,128)(2,1)} %bitcast_dynamic-update-slice_fusion.1, bf16[768,1,128]{2,0,1:T(8,128)(2,1)S(1)} %copy.59), kind=kLoop, calls=%fused_computation.8 | loop fusion | bytes 393216 | tf_op jit(solution)/shard_map/stack | solution.py:12
  14.2 5.1 %all-to-all-start = ((bf16[8,768,1,128]{3,1,2,0:T(8,128)(2,1)}), bf16[8,768,1,128]{3,1,2,0:T(8,128)(2,1)S(1)}, u32[]{:S(2)}, u32[]{:S(2)}) async-start(bf16[8,768,1,128]{3,1,2,0:T(8,128)(2,1)} %bitcast_dynamic-update-slice_fusion), calls=%async_computation | async-start | bytes 3145728 | tf_op jit(solution)/shard_map/all_to_all | solution.py:11
  19.3 0.8 %copy.50 = bf16[192,8,128]{2,0,1:T(8,128)(2,1)} copy(bf16[192,8,128]{2,1,0:T(8,128)(2,1)S(1)} %broadcast_multiply_fusion) | data formatting | bytes 786432 | tf_op jit(solution)/shard_map/mul | solution.py:36
  20.1 0.7 %convert_bitcast_fusion = f32[12]{0:T(128)S(1)} fusion(s32[12,8]{0,1:T(8,128)} %param.6, s32[]{:T(128)S(6)} %select_n.14), kind=kLoop, calls=%fused_computation.25 | loop fusion | flops 12 | bytes 100 | tf_op jit(solution)/shard_map/convert_element_type | solution.py:53
  20.9 19.4 %all-to-all-done = bf16[8,768,1,128]{3,1,2,0:T(8,128)(2,1)S(1)} async-done(((bf16[8,768,1,128]{3,1,2,0:T(8,128)(2,1)}), bf16[8,768,1,128]{3,1,2,0:T(8,128)(2,1)S(1)}, u32[]{:S(2)}, u32[]{:S(2)}) %all-to-all-start) | async-done | bytes 1572896 | tf_op jit(solution)/shard_map/all_to_all | solution.py:11
  40.3 3.5 %all-to-all-start.1 = ((bf16[192,8,128]{2,0,1:T(8,128)(2,1)}), bf16[192,8,128]{2,0,1:T(8,128)(2,1)S(1)}, u32[]{:S(2)}, u32[]{:S(2)}) async-start(bf16[192,8,128]{2,0,1:T(8,128)(2,1)} %copy.50), calls=%async_computation.1 | async-start | bytes 786432 | tf_op jit(solution)/shard_map/all_to_all | solution.py:51
  43.7 0.2 convert_reduce_fusion
  44.1 1.0 %fusion.2 = bf16[1536,1,128]{2,0,1:T(8,128)(2,1)} fusion(f32[4,2,192,1,128]{4,2,1,0,3:T(8,128)S(1)} %copy.49, f32[1536]{0:T(1024)S(1)} %broadcast_bitcast_fusion), kind=kLoop, calls=%fused_computation.7 | loop fusion | flops 589824 | bytes 1185792 | tf_op jit(solution)/shard_map/convert_element_type | solution.py:54
  45.1 6.9 %all-to-all-done.1 = bf16[192,8,128]{2,0,1:T(8,128)(2,1)S(1)} async-done(((bf16[192,8,128]{2,0,1:T(8,128)(2,1)}), bf16[192,8,128]{2,0,1:T(8,128)(2,1)S(1)}, u32[]{:S(2)}, u32[]{:S(2)}) %all-to-all-start.1) | async-done | bytes 393248 | tf_op jit(solution)/shard_map/all_to_all | solution.py:51
  52.0 1.2 %fusion = f32[1,128,128]{2,1,0:T(8,128)} fusion(f32[1,128,128]{2,1,0:T(8,128)S(1)} %copy-done.1, bf16[1536,128]{1,0:T(8,128)(2,1)S(1)} %bitcast.57, f32[1536,128]{1,0:T(8,128)S(1)} %bitcast.53), kind=kOutput, calls=%fused_computation.3 | convolution fusion | flops 302006272 | bytes 1310720 | tf_op jit(solution)/shard_map/rkb,rkc->kbc/dot_general | solution.py:55
  (7 shorter events, 0.2 us)
Async XLA Ops:
  0.6 5.5 %copy-start = (bf16[4,1,192,384]{3,2,1,0:T(8,128)(2,1)S(1)}, bf16[4,1,192,384]{3,2,1,0:T(8,128)(2,1)}, u32[]{:S(2)}) copy-start(bf16[4,1,192,384]{3,2,1,0:T(8,128)(2,1)} %param.4) | copy-start | bytes 1769476
  14.2 26.1 %all-to-all-start = ((bf16[8,768,1,128]{3,1,2,0:T(8,128)(2,1)}), bf16[8,768,1,128]{3,1,2,0:T(8,128)(2,1)S(1)}, u32[]{:S(2)}, u32[]{:S(2)}) async-start(bf16[8,768,1,128]{3,1,2,0:T(8,128)(2,1)} %bitcast_dynamic-update-slice_fusion), calls=%async_computation | async-start | bytes 3145728 | tf_op jit(solution)/shard_map/all_to_all | solution.py:11
  40.3 11.7 %all-to-all-start.1 = ((bf16[192,8,128]{2,0,1:T(8,128)(2,1)}), bf16[192,8,128]{2,0,1:T(8,128)(2,1)S(1)}, u32[]{:S(2)}, u32[]{:S(2)}) async-start(bf16[192,8,128]{2,0,1:T(8,128)(2,1)} %copy.50), calls=%async_computation.1 | async-start | bytes 786432 | tf_op jit(solution)/shard_map/all_to_all | solution.py:51
  44.0 8.0 %copy-start.1 = (f32[1,128,128]{2,1,0:T(8,128)S(1)}, f32[1,128,128]{2,1,0:T(8,128)}, u32[]{:S(2)}) copy-start(f32[1,128,128]{2,1,0:T(8,128)} %param.7) | copy-start | bytes 196612
